TPU v7x, 32 devices: a whole 2x2x4 slice. The times are simulated.
32 devices in a mesh: dp: 8 (over y, x, core), mp: 4 (over z).
Axes of the slice: x: 2, y: 2, z: 4, core: 2. Of those that a mesh axis runs over, the one named last changes fastest.
Arguments:
- patches: bfloat16 [8192, 768], P('dp'), may hold values from -6 to 6
- attention_gain: bfloat16 [768], replicated, may hold values from 0.5 to 1.5
- query_weight: bfloat16 [768, 768], P(None, 'mp'), may hold values from -0.0390625 to 0.0390625
- key_weight: bfloat16 [768, 768], P(None, 'mp'), may hold values from -0.3125 to 0.3125
- value_weight: bfloat16 [768, 768], P(None, 'mp'), may hold values from -0.21875 to 0.21875
- output_weight: bfloat16 [768, 768], P('mp'), may hold values from -0.875 to 0.875
- feedforward_gain: bfloat16 [768], replicated, may hold values from 0.5 to 1.5
- gate_weight: bfloat16 [768, 2048], P(None, 'mp'), may hold values from -0.21875 to 0.21875
- up_weight: bfloat16 [768, 2048], P(None, 'mp'), may hold values from -0.21875 to 0.21875
- down_weight: bfloat16 [2048, 768], P('mp'), may hold values from -0.25 to 0.25
- cotangent: bfloat16 [8192, 768], P('dp'), may hold values from -6 to 6
- grid_extent: int32 [8, 2], P('dp'), may hold values from 16 to 32, as said below
Outputs:
- layer_output: bfloat16 [8192, 768], P('dp')
- input_grad: float32 [8192, 768], P('dp')
- attention_grad: float32 [768], P('dp')
- query_grad: float32 [768, 768], P('dp', 'mp')
- key_grad: float32 [768, 768], P('dp', 'mp')
- value_grad: float32 [768, 768], P('dp', 'mp')
- output_grad: float32 [768, 768], P('mp', 'dp')
- feedforward_grad: float32 [768], P('dp')
- gate_grad: float32 [768, 2048], P('dp', 'mp')
- up_grad: float32 [768, 2048], P('dp', 'mp')
- down_grad: float32 [2048, 768], P('mp', 'dp')
Inputs may be any that keep to these rules, and one draw needn't show every extreme that they name: `grid_extent`: chart 0 has all 32 rows and columns.
All inputs are finite; a program needn't handle non-finite values.
Results may differ from a plain program's by a relative error of at most 0.015.
Values may be sent and summed in bfloat16 or wider, within the bound.
A program may use at most 128 MiB of HBM per device.

v0:
```python
import jax
import jax.numpy as jnp
from jax import lax
from jax.sharding import PartitionSpec as P

HEAD = 64


epsilon = 1e-06
masked_score = -1000000000.0


def rms_scale(values, gain_vec):
    return (
        values * lax.rsqrt(jnp.mean(values * values, axis=-1, keepdims=True) + epsilon) * gain_vec
    )


def patch_valid(grid_extent, length):
    position = jnp.arange(length, dtype=jnp.int32)
    return position[None, :] < grid_extent[:, 0:1] * grid_extent[:, 1:2]


def query_blocks(length):
    block_rows = min(512, length)
    return (block_rows, jnp.arange(length // block_rows, dtype=jnp.int32) * block_rows)


def block_scores(query_block, keys_all, key_bias):
    scores = jnp.einsum("qhd,khd->hqk", query_block, keys_all, preferred_element_type=jnp.float32)
    return scores + key_bias


def attend_chart(chart_item):
    queries, keys_all, values_all, key_ok = chart_item
    block_rows, starts = query_blocks(queries.shape[0])
    key_bias = jnp.where(key_ok, 0.0, masked_score).astype(jnp.float32)

    def one_block(start):
        query_block = lax.dynamic_slice_in_dim(queries, start, block_rows, 0)
        scores = block_scores(query_block, keys_all, key_bias)
        highest = jnp.max(scores, axis=-1, keepdims=True)
        logsum = highest + jnp.log(jnp.sum(jnp.exp(scores - highest), axis=-1, keepdims=True))
        probs = jnp.exp(scores - logsum).astype(jnp.bfloat16)
        context = jnp.einsum("hqk,khd->qhd", probs, values_all, preferred_element_type=jnp.float32)
        return (context.astype(jnp.bfloat16), logsum)

    context, logsum = lax.map(one_block, starts)
    return (context.reshape(queries.shape), logsum)


def attend_back(chart_item):
    queries, keys_all, values_all, key_ok, logsum, context_back = chart_item
    block_rows, starts = query_blocks(queries.shape[0])
    key_bias = jnp.where(key_ok, 0.0, masked_score).astype(jnp.float32)

    def one_block(carry, block_item):
        key_total, value_total = carry
        start, block_logsum = block_item
        query_block = lax.dynamic_slice_in_dim(queries, start, block_rows, 0)
        grad_block = lax.dynamic_slice_in_dim(context_back, start, block_rows, 0)
        probs_full = jnp.exp(block_scores(query_block, keys_all, key_bias) - block_logsum)
        value_total = value_total + jnp.einsum(
            "hqk,qhd->khd",
            probs_full.astype(jnp.bfloat16),
            grad_block,
            preferred_element_type=jnp.float32,
        )
        probs_back = jnp.einsum(
            "qhd,khd->hqk", grad_block, values_all, preferred_element_type=jnp.float32
        )
        score_back = probs_full * (
            probs_back - jnp.sum(probs_full * probs_back, axis=-1, keepdims=True)
        )
        score_back = score_back.astype(jnp.bfloat16)
        query_part = jnp.einsum(
            "hqk,khd->qhd", score_back, keys_all, preferred_element_type=jnp.float32
        )
        key_total = key_total + jnp.einsum(
            "hqk,qhd->khd", score_back, query_block, preferred_element_type=jnp.float32
        )
        return ((key_total, value_total), query_part.astype(jnp.bfloat16))

    zeros_keys = jnp.zeros(keys_all.shape, jnp.float32)
    (key_total, value_total), query_back = lax.scan(
        one_block, (zeros_keys, zeros_keys), (starts, logsum)
    )
    return (
        query_back.reshape(queries.shape),
        key_total.astype(jnp.bfloat16),
        value_total.astype(jnp.bfloat16),
    )


def layer_forward(inputs, weights, valid_mask, attention_total):
    (
        first_gain,
        query_weight,
        key_weight,
        value_weight,
        output_weight,
        second_gain,
        gate_weight,
        up_weight,
        down_weight,
    ) = weights
    rows_total = inputs.shape[0]
    charts = valid_mask.shape[0]
    length = rows_total // charts
    normed_one = rms_scale(inputs, first_gain).astype(jnp.bfloat16)

    def project(matrix):
        product = jnp.dot(normed_one, matrix, preferred_element_type=jnp.float32)
        return product.astype(jnp.bfloat16).reshape(charts, length, matrix.shape[1] // HEAD, HEAD)

    queries = project(query_weight)
    keys_all = project(key_weight)
    values_all = project(value_weight)
    context, logsum = lax.map(attend_chart, (queries, keys_all, values_all, valid_mask))
    context = context.reshape(rows_total, query_weight.shape[1])
    attention_out = attention_total(
        jnp.dot(context, output_weight, preferred_element_type=jnp.float32)
    )
    hidden = inputs + attention_out
    normed_two = rms_scale(hidden, second_gain).astype(jnp.bfloat16)
    gate_pre = jnp.dot(normed_two, gate_weight, preferred_element_type=jnp.float32)
    up_pre = jnp.dot(normed_two, up_weight, preferred_element_type=jnp.float32)
    mixed = (jax.nn.gelu(gate_pre, approximate=True) * up_pre).astype(jnp.bfloat16)
    return (
        normed_one,
        queries,
        keys_all,
        values_all,
        logsum,
        context,
        hidden,
        normed_two,
        gate_pre,
        up_pre,
        mixed,
    )


def gelu_product(gate_pre, up_pre):
    return jax.nn.gelu(gate_pre, approximate=True) * up_pre


def body(
    patches,
    attention_gain,
    query_weight,
    key_weight,
    value_weight,
    output_weight,
    feedforward_gain,
    gate_weight,
    up_weight,
    down_weight,
    cotangent,
    grid_extent,
):
    rows_total = patches.shape[0]
    charts = grid_extent.shape[0]
    length = rows_total // charts
    valid_mask = patch_valid(grid_extent, length)
    row_keep = valid_mask.reshape(rows_total, 1)
    inputs = patches.astype(jnp.float32)
    first_gain = attention_gain.astype(jnp.float32)
    second_gain = feedforward_gain.astype(jnp.float32)
    weights = (
        first_gain,
        query_weight,
        key_weight,
        value_weight,
        output_weight,
        second_gain,
        gate_weight,
        up_weight,
        down_weight,
    )

    def attention_total(partial_value):
        share = lax.psum_scatter(partial_value, "mp", scatter_dimension=0, tiled=True)
        return lax.all_gather(share, "mp", axis=0, tiled=True)

    def attention_repeat(partial_value):
        share = lax.psum_scatter(partial_value, "mp", scatter_dimension=0, tiled=True)
        return lax.all_gather(share, "mp", axis=0, tiled=True)

    first_pass = layer_forward(inputs, weights, valid_mask, attention_total)
    feedforward_share = lax.psum_scatter(
        jnp.dot(first_pass[10], down_weight, preferred_element_type=jnp.float32),
        "mp",
        scatter_dimension=0,
        tiled=True,
    )
    rows_here = feedforward_share.shape[0]
    row_start = lax.axis_index("mp") * rows_here
    hidden_here = lax.dynamic_slice_in_dim(first_pass[6], row_start, rows_here, 0)
    keep_here = lax.dynamic_slice_in_dim(row_keep, row_start, rows_here, 0)
    output_here = jnp.where(keep_here, hidden_here + feedforward_share, 0.0).astype(jnp.bfloat16)
    layer_output = lax.all_gather(output_here, "mp", axis=0, tiled=True)
    saved = layer_forward(inputs, weights, valid_mask, attention_repeat)
    (
        normed_one,
        queries,
        keys_all,
        values_all,
        logsum,
        context,
        hidden,
        normed_two,
        gate_pre,
        up_pre,
        mixed,
    ) = saved
    out_back = jnp.where(row_keep, cotangent.astype(jnp.float32), 0.0)
    out_low = out_back.astype(jnp.bfloat16)
    down_grad = jnp.einsum("rf,rd->fd", mixed, out_low, preferred_element_type=jnp.float32)
    mixed_back = jnp.einsum("rd,fd->rf", out_low, down_weight, preferred_element_type=jnp.float32)
    _, gelu_pull = jax.vjp(gelu_product, gate_pre, up_pre)
    gate_back, up_back = gelu_pull(mixed_back)
    gate_back = gate_back.astype(jnp.bfloat16)
    up_back = up_back.astype(jnp.bfloat16)
    gate_grad = jnp.einsum("rd,rf->df", normed_two, gate_back, preferred_element_type=jnp.float32)
    up_grad = jnp.einsum("rd,rf->df", normed_two, up_back, preferred_element_type=jnp.float32)
    normed_two_part = jnp.einsum(
        "rf,df->rd", gate_back, gate_weight, preferred_element_type=jnp.float32
    ) + jnp.einsum("rf,df->rd", up_back, up_weight, preferred_element_type=jnp.float32)
    normed_two_share = lax.psum_scatter(normed_two_part, "mp", scatter_dimension=0, tiled=True)
    normed_two_back = lax.all_gather(normed_two_share, "mp", axis=0, tiled=True)
    _, second_pull = jax.vjp(rms_scale, hidden, second_gain)
    hidden_part, second_gain_grad = second_pull(normed_two_back)
    hidden_back = out_back + hidden_part
    second_gain_grad, gate_grad, up_grad = (
        lax.psum_scatter(second_gain_grad, "dp", scatter_dimension=0, tiled=True),
        lax.psum_scatter(gate_grad, "dp", scatter_dimension=0, tiled=True),
        lax.psum_scatter(up_grad, "dp", scatter_dimension=0, tiled=True),
    )
    down_grad = lax.psum_scatter(down_grad, "dp", scatter_dimension=1, tiled=True)
    hidden_low = hidden_back.astype(jnp.bfloat16)
    output_grad = jnp.einsum("rc,rd->cd", context, hidden_low, preferred_element_type=jnp.float32)
    context_back = jnp.einsum(
        "rd,cd->rc", hidden_low, output_weight, preferred_element_type=jnp.float32
    )
    context_back = context_back.astype(jnp.bfloat16).reshape(queries.shape)
    query_back, key_back, value_back = lax.map(
        attend_back, (queries, keys_all, values_all, valid_mask, logsum, context_back)
    )
    features_here = query_weight.shape[1]
    query_back = query_back.reshape(rows_total, features_here)
    key_back = key_back.reshape(rows_total, features_here)
    value_back = value_back.reshape(rows_total, features_here)
    query_grad = jnp.einsum("rd,rc->dc", normed_one, query_back, preferred_element_type=jnp.float32)
    key_grad = jnp.einsum("rd,rc->dc", normed_one, key_back, preferred_element_type=jnp.float32)
    value_grad = jnp.einsum("rd,rc->dc", normed_one, value_back, preferred_element_type=jnp.float32)
    normed_one_part = (
        jnp.einsum("rc,dc->rd", query_back, query_weight, preferred_element_type=jnp.float32)
        + jnp.einsum("rc,dc->rd", key_back, key_weight, preferred_element_type=jnp.float32)
        + jnp.einsum("rc,dc->rd", value_back, value_weight, preferred_element_type=jnp.float32)
    )
    normed_one_share = lax.psum_scatter(normed_one_part, "mp", scatter_dimension=0, tiled=True)
    normed_one_back = lax.all_gather(normed_one_share, "mp", axis=0, tiled=True)
    _, first_pull = jax.vjp(rms_scale, inputs, first_gain)
    input_part, first_gain_grad = first_pull(normed_one_back)
    input_grad = hidden_back + input_part
    first_gain_grad, query_grad, key_grad, value_grad = (
        lax.psum_scatter(first_gain_grad, "dp", scatter_dimension=0, tiled=True),
        lax.psum_scatter(query_grad, "dp", scatter_dimension=0, tiled=True),
        lax.psum_scatter(key_grad, "dp", scatter_dimension=0, tiled=True),
        lax.psum_scatter(value_grad, "dp", scatter_dimension=0, tiled=True),
    )
    output_grad = lax.psum_scatter(output_grad, "dp", scatter_dimension=1, tiled=True)
    return (
        layer_output,
        input_grad,
        first_gain_grad,
        query_grad,
        key_grad,
        value_grad,
        output_grad,
        second_gain_grad,
        gate_grad,
        up_grad,
        down_grad,
    )


def solution(mesh):
    placed = (
        P("dp", None),
        P(),
        P(None, "mp"),
        P(None, "mp"),
        P(None, "mp"),
        P("mp", None),
        P(),
        P(None, "mp"),
        P(None, "mp"),
        P("mp", None),
        P("dp", None),
        P("dp", None),
    )
    return jax.shard_map(
        body,
        mesh=mesh,
        in_specs=placed,
        out_specs=(
            P("dp", None),
            P("dp", None),
            P("dp"),
            P("dp", "mp"),
            P("dp", "mp"),
            P("dp", "mp"),
            P("mp", "dp"),
            P("dp"),
            P("dp", "mp"),
            P("dp", "mp"),
            P("mp", "dp"),
        ),
        check_vma=False,
    )
```

profile of v0, /device:TPU:0, one launch (start us, length us, event | category | flops | bytes accessed | tf_op | source)
XLA Modules:
  0.0 994.8 jit_solution(6283610246792495754)
XLA Ops:
  16.5 12.8 %while.67 = (s32[]{:T(128)}, bf16[2,512,3,64]{1,3,2,0:T(8,128)(2,1)S(1)}, f32[2,3,512,1]{2,1,3,0:T(4,128)S(1)}, s32[2]{0:T(128)S(1)}, bf16[1024,3,64]{0,2,1:T(8,...) while((s32[]{:T(128)}, ...), condition=%wide.region_11.12_spmd.clone, body=%wide.region_8.11_spmd.clone.sunk | while | flops 415334912 | bytes 20129972 | solution.py:48
  33.3 63.1 %reduce-scatter.19.cloned.1.call-done = f32[256,768]{1,0:T(8,128)} async-done(((f32[1024,768]{1,0:T(8,128)}), f32[256,768]{1,0:T(8,128)}) %reduce-scatter.19.cloned.1.call-update) | async-done | bytes 786448 | tf_op jit(solution)/shard_map/reduce_scatter | solution.py:187
  96.5 65.0 %all-gather.10.cloned.1.call-done = f32[1024,768]{1,0:T(8,128)} async-done(((f32[256,768]{1,0:T(8,128)}), f32[1024,768]{1,0:T(8,128)}) %all-gather.10.cloned.1.call-update) | async-done | bytes 3145744 | tf_op jit(solution)/shard_map/all_gather | solution.py:188
  169.1 2.8 multiply_convert_fusion.4
  173.1 2.7 convolution_add_fusion
  175.9 59.0 %reduce-scatter.21.cloned.1.call-done = f32[256,768]{1,0:T(8,128)} async-done(((f32[1024,768]{1,0:T(8,128)}), f32[256,768]{1,0:T(8,128)}) %reduce-scatter.21.cloned.1.call-update) | async-done | bytes 786448 | tf_op jit(solution)/shard_map/reduce_scatter | solution.py:230
  235.2 64.7 %all-gather.12.cloned.1.call-done = f32[1024,768]{1,0:T(8,128)} async-done(((f32[256,768]{1,0:T(8,128)}), f32[1024,768]{1,0:T(8,128)}) %all-gather.12.cloned.1.call-update) | async-done | bytes 3145744 | tf_op jit(solution)/shard_map/all_gather | solution.py:231
  299.9 4.6 multiply_reduce_fusion.1
  310.4 24.8 %while.68 = (s32[]{:T(128)}, f32[1024,3,64]{0,2,1:T(8,128)S(1)}, f32[1024,3,64]{0,2,1:T(8,128)}, bf16[2,512,3,64]{1,3,2,0:T(8,128)(2,1)}, s32[2]{0:T(128)}, /*in...) while((s32[]{:T(128)}, f32[1024,3,64]{0,2,1:T(8,128)S(1)}, ...), condition=%wide.region_18.19_spmd.clone, body=%wide.region_16.18_spmd.clone.sunk | while | flops 1026392576 | bytes 66714016 | solution.py:85
  342.1 14.3 %while.66 = (s32[]{:T(128)}, bf16[2,512,3,64]{1,3,2,0:T(8,128)(2,1)}, s32[2]{0:T(128)S(1)}, bf16[1024,3,64]{0,2,1:T(8,128)(2,1)S(1)}, bf16[1024,3,64]{0,2,1:T(8,...) while((s32[]{:T(128)}, ...), condition=%wide.region_4.5_spmd.clone, body=%wide.region_1.4_spmd.clone.sunk | while | flops 415334912 | bytes 23261408 | solution.py:48
  357.9 3.3 fusion.97
  361.2 38.9 %reduce-scatter.23.cloned.1.call-done = f32[256,768]{1,0:T(8,128)} async-done(((f32[1024,768]{1,0:T(8,128)}), f32[256,768]{1,0:T(8,128)}) %reduce-scatter.23.cloned.1.call-update) | async-done | bytes 786448 | tf_op jit(solution)/shard_map/reduce_scatter | solution.py:262
  400.2 63.0 %reduce-scatter.15.cloned.1.call-done = f32[256,768]{1,0:T(8,128)} async-done(((f32[1024,768]{1,0:T(8,128)}), f32[256,768]{1,0:T(8,128)}) %reduce-scatter.15.cloned.1.call-update) | async-done | bytes 786448 | tf_op jit(solution)/shard_map/reduce_scatter | solution.py:183
  463.2 65.1 %all-gather.14.cloned.1.call-done = f32[1024,768]{1,0:T(8,128)} async-done(((f32[256,768]{1,0:T(8,128)}), f32[1024,768]{1,0:T(8,128)}) %all-gather.14.cloned.1.call-update) | async-done | bytes 3145744 | tf_op jit(solution)/shard_map/all_gather | solution.py:263
  528.3 3.0 fusion.50
  531.3 60.7 %all-gather.6.cloned.1.call-done = f32[1024,768]{1,0:T(8,128)} async-done(((f32[256,768]{1,0:T(8,128)}), f32[1024,768]{1,0:T(8,128)}) %all-gather.6.cloned.1.call-update) | async-done | bytes 3145744 | tf_op jit(solution)/shard_map/all_gather | solution.py:184
  592.0 5.6 multiply_reduce_fusion.4
  601.7 6.3 fusion.72
  608.9 3.5 convolution_bitcast_fusion.1
  612.6 54.5 %reduce-scatter.17.cloned.1.call-done = f32[256,768]{1,0:T(8,128)} async-done(((f32[1024,768]{1,0:T(8,128)}), f32[256,768]{1,0:T(8,128)}) %reduce-scatter.17.cloned.1.call-update) | async-done | bytes 786448 | tf_op jit(solution)/shard_map/reduce_scatter | solution.py:191
  669.6 5.5 fusion.73
  675.2 3.4 fusion.107
  678.7 4.1 fusion.108
  688.8 16.3 %reduce-scatter.37.cloned.1.call-done = f32[96,192]{1,0:T(8,128)} async-done(((f32[768,192]{1,0:T(8,128)}), f32[96,192]{1,0:T(8,128)}) %reduce-scatter.37.cloned.1.call-update) | async-done | bytes 73744
  706.7 12.6 %all-reduce.2 = (f32[768]{0:T(1024)S(1)}, f32[768]{0:T(1024)S(1)}) all-reduce(f32[768]{0:T(1024)S(1)} %get-tuple-element.302, f32[768]{0:T(1024)S(1)} %copy-done.60), channel_id=7, replica_groups=mesh['dp'=8,'mp'=4] {'dp'}, use_global_device_ids=true, to_apply=%region_22.23.clone | all-reduce | flops 1536 | bytes 12288
  720.5 23.3 %all-gather.8.cloned.1.call-done = bf16[1024,768]{1,0:T(8,128)(2,1)} async-done(((bf16[256,768]{1,0:T(8,128)(2,1)}), bf16[1024,768]{1,0:T(8,128)(2,1)}) %all-gather.8.cloned.1.call-update) | async-done | bytes 1572880 | tf_op jit(solution)/shard_map/all_gather | solution.py:202
  743.8 41.1 %reduce-scatter.35.cloned.1.call-done = f32[512,96]{0,1:T(8,128)} async-done(((f32[512,768]{0,1:T(8,128)}), f32[512,96]{0,1:T(8,128)}) %reduce-scatter.35.cloned.1.call-update) | async-done | bytes 196624 | tf_op jit(solution)/shard_map/reduce_scatter | solution.py:240
  784.9 42.4 %reduce-scatter.31.cloned.1.call-done = f32[96,512]{1,0:T(8,128)} async-done(((f32[768,512]{1,0:T(8,128)}), f32[96,512]{1,0:T(8,128)}) %reduce-scatter.31.cloned.1.call-update) | async-done | bytes 196624 | tf_op jit(solution)/shard_map/reduce_scatter | solution.py:237
  827.2 42.2 %reduce-scatter.33.cloned.1.call-done = f32[96,512]{1,0:T(8,128)} async-done(((f32[768,512]{1,0:T(8,128)}), f32[96,512]{1,0:T(8,128)}) %reduce-scatter.33.cloned.1.call-update) | async-done | bytes 196624 | tf_op jit(solution)/shard_map/reduce_scatter | solution.py:238
  869.4 38.6 %reduce-scatter.29.cloned.1.call-done = f32[96,192]{1,0:T(8,128)} async-done(((f32[768,192]{1,0:T(8,128)}), f32[96,192]{1,0:T(8,128)}) %reduce-scatter.29.cloned.1.call-update) | async-done | bytes 73744 | tf_op jit(solution)/shard_map/reduce_scatter | solution.py:271
  908.0 38.6 %reduce-scatter.25.cloned.1.call-done = f32[96,192]{1,0:T(8,128)} async-done(((f32[768,192]{1,0:T(8,128)}), f32[96,192]{1,0:T(8,128)}) %reduce-scatter.25.cloned.1.call-update) | async-done | bytes 73744 | tf_op jit(solution)/shard_map/reduce_scatter | solution.py:269
  946.6 38.6 %reduce-scatter.27.cloned.1.call-done = f32[96,192]{1,0:T(8,128)} async-done(((f32[768,192]{1,0:T(8,128)}), f32[96,192]{1,0:T(8,128)}) %reduce-scatter.27.cloned.1.call-update) | async-done | bytes 73744 | tf_op jit(solution)/shard_map/reduce_scatter | solution.py:270
  (289 shorter events, 93.4 us)
Async XLA Ops:
  7.2 159.5 %copy-start = (bf16[768,512]{1,0:T(8,128)(2,1)S(1)}, bf16[768,512]{1,0:T(8,128)(2,1)}, u32[]{:S(2)}) copy-start(bf16[768,512]{1,0:T(8,128)(2,1)} %param.26) | copy-start | bytes 2359300
  7.2 5.9 copy-start.41
  7.2 89.2 %reduce-scatter.19.cloned.1.call-start = ((), (), s32[]{:S(2)}) async-start(), calls=%async_computation.16 | async-start | bytes 3932160 | tf_op jit(solution)/shard_map/reduce_scatter | solution.py:187
  16.5 14.5 %copy-start.29 = (bf16[192,768]{1,0:T(8,128)(2,1)S(1)}, bf16[192,768]{1,0:T(8,128)(2,1)}, u32[]{:S(2)}) copy-start(bf16[192,768]{1,0:T(8,128)(2,1)} %param.23) | copy-start | bytes 884740
  31.0 65.5 %copy-start.61 = (bf16[768]{0:T(1024)(128)(2,1)S(1)}, bf16[768]{0:T(1024)(128)(2,1)}, u32[]{:S(2)}) copy-start(bf16[768]{0:T(1024)(128)(2,1)} %param.24) | copy-start | bytes 4612
  31.0 130.6 %copy-start.1 = (bf16[1024,768]{1,0:T(8,128)(2,1)S(1)}, bf16[1024,768]{1,0:T(8,128)(2,1)}, u32[]{:S(2)}) copy-start(bf16[1024,768]{1,0:T(8,128)(2,1)} %param.18) | copy-start | bytes 4718596
  33.3 128.2 %all-gather.10.cloned.1.call-start = ((), (), s32[]{:S(2)}) async-start(), calls=%async_computation.17 | async-start | bytes 3932160 | tf_op jit(solution)/shard_map/all_gather | solution.py:188
  96.4 138.5 %reduce-scatter.21.cloned.1.call-start = ((), (), s32[]{:S(2)}) async-start(), calls=%async_computation.18 | async-start | bytes 3932160 | tf_op jit(solution)/shard_map/reduce_scatter | solution.py:230
  96.5 68.4 %copy-start.47 = (f32[768]{0:T(1024)}, f32[768]{0:T(1024)S(1)}, u32[]{:S(2)}) copy-start(f32[768]{0:T(1024)S(1)} %convert_element_type.102) | copy-start | bytes 9220
  96.5 71.1 %copy-start.62 = (pred[1024]{0:T(1024)(128)(4,1)}, pred[1024]{0:T(1024)(128)(4,1)S(1)}, u32[]{:S(2)}) copy-start(pred[1024]{0:T(1024)(128)(4,1)S(1)} %iota_compare_fusion.3) | copy-start | bytes 3076
  175.9 124.0 %all-gather.12.cloned.1.call-start = ((), (), s32[]{:S(2)}) async-start(), calls=%async_computation.19 | async-start | bytes 3932160 | tf_op jit(solution)/shard_map/all_gather | solution.py:231
  235.0 165.1 %reduce-scatter.23.cloned.1.call-start = ((), (), s32[]{:S(2)}) async-start(), calls=%async_computation.20 | async-start | bytes 3932160 | tf_op jit(solution)/shard_map/reduce_scatter | solution.py:262
  341.0 122.1 %reduce-scatter.15.cloned.1.call-start = ((), (), s32[]{:S(2)}) async-start(), calls=%async_computation.12 | async-start | bytes 3932160 | tf_op jit(solution)/shard_map/reduce_scatter | solution.py:183
  361.1 167.2 %copy-start.51 = (f32[768]{0:T(1024)S(1)}, f32[768]{0:T(1024)}, u32[]{:S(2)}) copy-start(f32[768]{0:T(1024)} %copy-done.50) | copy-start | bytes 9220
  361.1 167.2 %copy-start.53 = (f32[1024]{0:T(1024)S(1)}, f32[1024]{0:T(1024)}, u32[]{:S(2)}) copy-start(f32[1024]{0:T(1024)} %copy-done.52) | copy-start | bytes 12292
  361.2 167.1 %all-gather.14.cloned.1.call-start = ((), (), s32[]{:S(2)}) async-start(), calls=%async_computation.21 | async-start | bytes 3932160 | tf_op jit(solution)/shard_map/all_gather | solution.py:263
  400.1 131.2 %copy-start.57 = (f32[1024]{0:T(1024)S(1)}, f32[1024]{0:T(1024)}, u32[]{:S(2)}) copy-start(f32[1024]{0:T(1024)} %copy-done.56) | copy-start | bytes 12292
  400.1 191.9 %all-gather.6.cloned.1.call-start = ((), (), s32[]{:S(2)}) async-start(), calls=%async_computation.13 | async-start | bytes 3932160 | tf_op jit(solution)/shard_map/all_gather | solution.py:184
  463.2 203.9 %reduce-scatter.17.cloned.1.call-start = ((), (), s32[]{:S(2)}) async-start(), calls=%async_computation.14 | async-start | bytes 3932160 | tf_op jit(solution)/shard_map/reduce_scatter | solution.py:191
  531.3 68.0 %copy-start.28 = (bf16[768,512]{1,0:T(8,128)(2,1)S(1)}, bf16[768,512]{1,0:T(8,128)(2,1)}, u32[]{:S(2)}) copy-start(bf16[768,512]{1,0:T(8,128)(2,1)} %param.25) | copy-start | bytes 2359300
  531.3 68.0 %copy-start.49 = (f32[768]{0:T(1024)S(1)}, f32[768]{0:T(1024)}, u32[]{:S(2)}) copy-start(f32[768]{0:T(1024)} %copy-done.47) | copy-start | bytes 9220
  608.0 61.6 %copy-start.64 = (pred[1024]{0:T(1024)(128)(4,1)S(1)}, pred[1024]{0:T(1024)(128)(4,1)}, u32[]{:S(2)}) copy-start(pred[1024]{0:T(1024)(128)(4,1)} %copy-done.62) | copy-start | bytes 3076
  608.0 97.1 %reduce-scatter.37.cloned.1.call-start = ((), (), s32[]{:S(2)}) async-start(), calls=%async_computation.28 | async-start | bytes 884736
  612.5 131.3 %all-gather.8.cloned.1.call-start = ((), (), s32[]{:S(2)}) async-start(), calls=%async_computation.15 | async-start | bytes 1966080 | tf_op jit(solution)/shard_map/all_gather | solution.py:202
  669.3 5.9 copy-start.36
  669.3 115.6 %reduce-scatter.35.cloned.1.call-start = ((), (), s32[]{:S(2)}) async-start(), calls=%async_computation.27 | async-start | bytes 1769472 | tf_op jit(solution)/shard_map/reduce_scatter | solution.py:240
  675.2 152.1 %reduce-scatter.31.cloned.1.call-start = ((), (), s32[]{:S(2)}) async-start(), calls=%async_computation.25 | async-start | bytes 1769472 | tf_op jit(solution)/shard_map/reduce_scatter | solution.py:237
  678.6 190.8 %reduce-scatter.33.cloned.1.call-start = ((), (), s32[]{:S(2)}) async-start(), calls=%async_computation.26 | async-start | bytes 1769472 | tf_op jit(solution)/shard_map/reduce_scatter | solution.py:238
  682.8 225.2 %reduce-scatter.29.cloned.1.call-start = ((), (), s32[]{:S(2)}) async-start(), calls=%async_computation.24 | async-start | bytes 884736 | tf_op jit(solution)/shard_map/reduce_scatter | solution.py:271
  684.4 22.3 %copy-start.60 = (f32[768]{0:T(1024)S(1)}, f32[768]{0:T(1024)}, u32[]{:S(2)}) copy-start(f32[768]{0:T(1024)} %get-tuple-element.300) | copy-start | bytes 9220
  684.4 262.2 %reduce-scatter.25.cloned.1.call-start = ((), (), s32[]{:S(2)}) async-start(), calls=%async_computation.22 | async-start | bytes 884736 | tf_op jit(solution)/shard_map/reduce_scatter | solution.py:269
  686.0 299.2 %reduce-scatter.27.cloned.1.call-start = ((), (), s32[]{:S(2)}) async-start(), calls=%async_computation.23 | async-start | bytes 884736 | tf_op jit(solution)/shard_map/reduce_scatter | solution.py:270
  (66 other events, 141.5 us)
Sparse Core Ops, SparseCore 0:
  33.4 62.9 reduce-scatter.18
  98.0 63.4 all-gather.9
  176.0 58.8 reduce-scatter.20
  236.4 63.4 all-gather.11
  341.2 58.8 reduce-scatter.22
  402.8 60.2 reduce-scatter.14
  464.7 63.5 all-gather.13
  529.8 62.1 all-gather.5
  608.1 58.8 reduce-scatter.16
  670.0 35.0 reduce-scatter.36
  706.7 37.0 all-gather.7
  747.5 37.3 reduce-scatter.34
  788.7 38.4 reduce-scatter.30
  830.9 38.4 reduce-scatter.32
  873.0 34.9 reduce-scatter.28
  911.6 34.9 reduce-scatter.24
  950.2 34.9 reduce-scatter.26
where the time goes:
time: 1000 us; the launch traced here: 995 us
  waiting for transfers between devices  815 us (82%)
  matrix products  75.7 us (8%)
  other arithmetic  32.9 us (3%)
  local copies, waits for them, and re-layouts  27.9 us (3%)
  between operations  17.2 us (2%)
  blocking collectives  12.6 us (1%)
  loops' own time  12.1 us (1%)
    all_gather x1, waiting for transfers between devices, body(): normed_one_back = lax.all_gather(normed_one_share, 'mp', axis=0, tiled=True)  65.1 us
    all_gather x1, waiting for transfers between devices, attention_repeat(): return lax.all_gather(share, 'mp', axis=0, tiled=True)  65 us
    all_gather x1, waiting for transfers between devices, body(): normed_two_back = lax.all_gather(normed_two_share, 'mp', axis=0, tiled=True)  64.7 us
    reduce_scatter x1, waiting for transfers between devices, attention_repeat(): lax.psum_scatter(partial_value, 'mp', scatter_dimension=0, tiled=True)  63.1 us
    reduce_scatter x1, waiting for transfers between devices, attention_total(): lax.psum_scatter(partial_value, 'mp', scatter_dimension=0, tiled=True)  63 us
    all_gather x1, waiting for transfers between devices, attention_total(): return lax.all_gather(share, 'mp', axis=0, tiled=True)  60.7 us
    reduce_scatter x1, waiting for transfers between devices, body(): lax.psum_scatter(normed_two_part, 'mp', scatter_dimension=0, tiled=True)  59 us
    reduce_scatter x1, waiting for transfers between devices, body(): lax.psum_scatter(jnp.dot(first_pass[10], down_weight, preferred_element_t...  54.5 us
  transfers between devices with their start and end apart: 17, of which 17 were waited for; matrix products, arithmetic and copies ran while one was open for 4% of the time, Pallas kernels for 0%

commit v1 on v0

v1 whole, which is shorter than its diff:
```python
import functools

import jax
import jax.numpy as jnp
from jax import lax
from jax.experimental import pallas as pl
from jax.experimental.pallas import tpu as pltpu
from jax.sharding import PartitionSpec as P

HEAD = 64
EPSILON = 1e-06
MASKED = -1000000000.0
MESH = pl.DeviceIdType.MESH
f32 = jnp.float32
bf16 = jnp.bfloat16
GROUP = 8
VMEM_LIMIT = 61 << 20


def dot(left, right, left_dim, right_dim):
    return lax.dot_general(
        left, right, (((left_dim,), (right_dim,)), ((), ())), preferred_element_type=f32
    )


def flip(value, bits):
    result = value
    for bit in (1, 2, 4):
        if bits & bit:
            result = result + bit - 2 * bit * ((value // bit) % 2)
    return result


def cross(value, mask):
    low = (value + mask) % 2
    return low + 2 * ((value // 2 + mask // 2) % 2)


def aligned(value, multiple):
    return pl.multiple_of(value, multiple)


class Gather:
    KINDS = 5

    def __init__(self, sources, places, send_z, recv_z, send_x, recv_x, send_c, recv_c):
        self.dp, self.mp = lax.axis_index("dp"), lax.axis_index("mp")
        self.core = self.dp % 2
        self.chip = (self.dp // 2) % 4
        self.sources, self.places = sources, places
        self.sems = (send_z, recv_z, send_x, recv_x, send_c, recv_c)
        self.sends = []

    def part(self, ref, lead, quarter, half):
        rows, columns = ref.shape[-2] // 4, ref.shape[-1] // 2
        window = (
            pl.ds(aligned(quarter * rows, 16), rows),
            pl.ds(aligned(half * columns, 128), columns),
        )
        middle = (slice(None),) * (len(ref.shape) - 2 - len(lead))
        return ref.at[(*lead, *middle, *window)]

    def place(self, kind, shard, quarter, half):
        return self.part(self.places[kind], (shard,), quarter, half)

    def copy(self, source, target, send, recv, dp, mp):
        return pltpu.make_async_remote_copy(
            src_ref=source,
            dst_ref=target,
            send_sem=send,
            recv_sem=recv,
            device_id=(dp, mp),
            device_id_type=MESH,
        )

    def start(self, make, *which):
        make(*which).start()
        self.sends.append((make, which))

    def arrived(self, target, send, recv):
        self.copy(target, target, send, recv, self.dp, self.mp).wait_recv()

    def along_mp(self, kind, k):
        send_z, recv_z = self.sems[:2]
        target = self.place(kind, self.mp, self.chip, self.core)
        source = target
        if self.sources[kind] is not None:
            source = self.part(self.sources[kind], (), self.chip, self.core)
        peer = flip(self.mp, k)
        return self.copy(source, target, send_z.at[kind, k], recv_z.at[kind, k], self.dp, peer)

    def to_core(self, kind, k, j):
        piece = self.place(kind, flip(self.mp, k), flip(self.chip, j), self.core)
        send_c, recv_c = self.sems[4:]
        peer = flip(self.dp, 1)
        return self.copy(piece, piece, send_c.at[kind, k, j], recv_c.at[kind, k, j], peer, self.mp)

    def to_chip(self, kind, k, j):
        send_x, recv_x = self.sems[2:4]
        quarter, peer = self.chip, flip(self.dp, 2 * j)
        if j == 3:
            from_y, from_x = flip(self.chip, 2), flip(self.chip, 1)
            to_x, to_y = flip(self.dp, 2), flip(self.dp, 4)
            quarter = from_y + self.core * (from_x - from_y)
            peer = to_x + self.core * (to_y - to_x)
        piece = self.place(kind, flip(self.mp, k), quarter, self.core)
        return self.copy(piece, piece, send_x.at[kind, k, j], recv_x.at[kind, k, j], peer, self.mp)

    def to_chips(self, kind, k):
        send_z, recv_z = self.sems[:2]
        piece = self.place(kind, flip(self.mp, k), self.chip, self.core)
        self.arrived(piece, send_z.at[kind, k], recv_z.at[kind, k])
        self.start(self.to_chip, kind, k, 1)
        self.start(self.to_chip, kind, k, 2)
        self.start(self.to_core, kind, k, 0)

    def to_corner(self, kind, k):
        send_x, recv_x = self.sems[2:4]
        for j in (1, 2):
            piece = self.place(kind, flip(self.mp, k), flip(self.chip, j), self.core)
            self.arrived(piece, send_x.at[kind, k, j], recv_x.at[kind, k, j])
        self.start(self.to_chip, kind, k, 3)
        self.start(self.to_core, kind, k, 1)
        self.start(self.to_core, kind, k, 2)

    def last_core(self, kind, k):
        send_x, recv_x = self.sems[2:4]
        piece = self.place(kind, flip(self.mp, k), flip(self.chip, 3), self.core)
        self.arrived(piece, send_x.at[kind, k, 3], recv_x.at[kind, k, 3])
        self.start(self.to_core, kind, k, 3)

    def settled(self, kind, k):
        send_c, recv_c = self.sems[4:]
        for j in range(4):
            piece = self.place(kind, flip(self.mp, k), flip(self.chip, j), 1 - self.core)
            self.arrived(piece, send_c.at[kind, k, j], recv_c.at[kind, k, j])

    def schedule(self, jobs, window=8, start=3.0, pace=2.6, lags=(5.0, 10.0, 12.0)):
        for job in jobs[:window]:
            self.start(self.along_mp, *job)

        def first(i):
            self.to_chips(*jobs[i])
            if i + window < len(jobs):
                self.start(self.along_mp, *jobs[i + window])

        steps = []
        clock = start
        for i, job in enumerate(jobs):
            clock += 0.37 * pace if job[0] == 1 else pace
            steps.append((clock, functools.partial(first, i), job, False))
            later = (self.to_corner, self.last_core, self.settled)
            for lag, step in zip(lags, later):
                steps.append((clock + lag, functools.partial(step, *job), job, step == later[-1]))
        return sorted(steps, key=lambda step: step[0])

    def finish(self):
        for make, which in self.sends:
            make(*which).wait_send()


def announce(devices):
    semaphore = pltpu.get_barrier_semaphore()
    for device in devices:
        pl.semaphore_signal(semaphore, inc=1, device_id=device, device_id_type=MESH)
    return semaphore


def row_keep(count, first, rows):
    return lax.broadcasted_iota(jnp.int32, (rows, 1), 0) + first < count


def project(weights_ref, normed_ref, out_ref, shard):
    parts, features, depth = weights_ref.shape[1:]
    rows = normed_ref.shape[0]
    block = 256

    def step(i, _):
        at = pl.ds(aligned(i * block, block), block)
        weights = weights_ref[shard].reshape(parts * features, depth)
        out_ref[shard, :, at] = dot(weights, normed_ref[at, :], 1, 1).astype(bf16)
        return 0

    lax.fori_loop(0, rows // block, step, 0)


def attend(qkv_ref, shard, head, count, probs_ref, context_ref, scale_ref, scores, keys, local_heads, pause):
    rows = qkv_ref.shape[2]
    width = local_heads * HEAD
    block, chunk, group = 256, 128, 64
    at = pl.ds(aligned(head * HEAD, HEAD), HEAD)
    number = shard * local_heads + head
    context_at = pl.ds(aligned(number * HEAD, HEAD), HEAD)
    masked = jnp.where(row_keep(count, 0, rows), 0.0, MASKED)
    first_lane = lax.broadcasted_iota(jnp.int32, (rows, HEAD), 1) == 0
    keys[:, :HEAD] = qkv_ref[shard, pl.ds(aligned(width + head * HEAD, HEAD), HEAD), :].T
    keys[:, HEAD:] = jnp.where(first_lane, masked, 0.0).astype(bf16)
    queries = jnp.concatenate([qkv_ref[shard, at, :], jnp.ones((HEAD, rows), bf16)], axis=0)
    values = qkv_ref[shard, pl.ds(aligned(2 * width + head * HEAD, HEAD), HEAD), :]
    values = jnp.concatenate([values, jnp.ones((16, rows), bf16)], axis=0)
    blocks = rows // block
    highest = None
    for i in range(blocks + 1):
        ahead = None
        for first in range(0, rows, chunk):
            part = slice(first, first + chunk)
            if i < blocks:
                product = dot(keys[part, :], queries[:, i * block : (i + 1) * block], 1, 0)
                scores[i % 2, part, :] = product
                top = jnp.max(product.reshape(chunk // group, group, block), axis=0)
                ahead = top if ahead is None else jnp.maximum(ahead, top)
            if i > 0:
                weights = jnp.exp(scores[(i - 1) % 2, part, :] - highest)
                probs_ref[part, (i - 1) * block : i * block] = weights.astype(bf16)
        if i > 0:
            columns = slice((i - 1) * block, i * block)
            context = dot(values, probs_ref[:, columns], 1, 0)
            scale = 1.0 / context[HEAD : HEAD + 1]
            context_ref[context_at, columns] = (context[:HEAD] * scale).astype(bf16)
            scale_ref[number, :, columns] = scale
        if i < blocks:
            highest = jnp.max(ahead, axis=0, keepdims=True)
            pause(0.4)


def gelu_parts(gate):
    root = 0.7978845608028654
    square = gate * gate
    bend = jnp.tanh(gate * (root + (root * 0.044715) * square))
    half = 0.5 + 0.5 * bend
    slope = half + (0.5 * gate) * (1.0 - bend * bend) * (root + (3 * root * 0.044715) * square)
    return gate * half, slope


def attend_back(qkv_ref, grad_ref, shard, head, probs, context_back, delta, score_back, local_heads):
    rows = qkv_ref.shape[2]
    width = local_heads * HEAD
    block = 256
    head_at = pl.ds(aligned(head * HEAD, HEAD), HEAD)
    key_at = pl.ds(aligned(width + head * HEAD, HEAD), HEAD)
    value_at = pl.ds(aligned(2 * width + head * HEAD, HEAD), HEAD)
    number = shard * local_heads + head
    upstream = context_back[pl.ds(aligned(number * HEAD, HEAD), HEAD), :]
    queries, keys = qkv_ref[shard, head_at, :], qkv_ref[shard, key_at, :]
    high = delta[number].astype(bf16)
    low = (delta[number] - high.astype(f32)).astype(bf16)
    right = jnp.concatenate([upstream, high, low, jnp.zeros((14, rows), bf16)], axis=0)
    lane = lax.broadcasted_iota(jnp.int32, (rows, 16), 1)
    minus = jnp.where(lane < 2, -1.0, 0.0).astype(bf16)
    left = jnp.concatenate([qkv_ref[shard, value_at, :].T, minus], axis=1)
    for first in range(0, rows, block):
        part = slice(first, first + block)
        for i in range(0, rows, block):
            columns = slice(i, i + block)
            change = dot(left[part], right[:, columns], 1, 0)
            score_back[part, columns] = (probs[part, columns].astype(f32) * change).astype(bf16)
        grad_ref[shard, value_at, part] = dot(upstream, probs[part, :], 1, 1).astype(bf16)
        grad_ref[shard, key_at, part] = dot(queries, score_back[part, :], 1, 1).astype(bf16)
    grad_ref[shard, head_at, :] = dot(keys, score_back[...], 1, 0).astype(bf16)


class Reduce:
    def __init__(self, local, from_core, from_chips, total, sems):
        self.local, self.from_core = local, from_core
        self.from_chips, self.total, self.sems = from_chips, total, sems
        self.dp, self.mp = lax.axis_index("dp"), lax.axis_index("mp")
        self.core, self.chip = self.dp % 2, (self.dp // 2) % 4

    def copy(self, j):
        if j == 0:
            source, target, peer = self.local.at[:, 1 - self.core], self.from_core, flip(self.dp, 1)
        else:
            source, target = self.local.at[flip(self.chip, j), self.core], self.from_chips.at[j - 1]
            peer = flip(self.dp, 2 * j)
        return pltpu.make_async_remote_copy(
            src_ref=source,
            dst_ref=target,
            send_sem=self.sems.at[0, j],
            recv_sem=self.sems.at[1, j],
            device_id=(peer, self.mp),
            device_id_type=MESH,
        )

    def begin(self):
        self.copy(0).start()

    def middle(self):
        self.copy(0).wait()
        for j in (1, 2, 3, 0):
            chip = flip(self.chip, j)
            part = self.local[chip, self.core].astype(f32) + self.from_core[chip].astype(f32)
            if j == 0:
                self.total[...] = part
            else:
                self.local[chip, self.core] = part.astype(bf16)
                self.copy(j).start()

    def end(self):
        for j in (1, 2, 3):
            self.copy(j).wait()
        first, second, third = (self.from_chips[i].astype(f32) for i in range(3))
        self.total[...] += first + second + third


def main_kernel(
    extent,
    inputs,
    first_gain,
    second_gain,
    upstream,
    query_source,
    key_source,
    value_source,
    output_source,
    gate_source,
    up_source,
    down_source,
    layer_output,
    probs_out,
    grads_out,
    weights_out,
    hidden_out,
    wide_total,
    narrow_total,
    gains_total,
    attention_weights,
    output_weights,
    gate_weights,
    up_weights,
    down_weights,
    qkv,
    context,
    normed_one,
    normed_two,
    out_low,
    hidden,
    scale,
    delta,
    context_back,
    wide_grad,
    narrow_grad,
    wide_core,
    wide_chips,
    narrow_core,
    narrow_chips,
    gains_own,
    gains_in,
    own_weights,
    local_sem,
    probs_sem,
    out_sem,
    grads_sem,
    wide_sem,
    narrow_sem,
    gains_sem,
    send_z,
    recv_z,
    send_x,
    recv_x,
    send_c,
    recv_c,
):
    dp, mp = lax.axis_index("dp"), lax.axis_index("mp")
    shards = attention_weights.shape[0]
    rows, depth = inputs.shape
    features = output_weights.shape[1]
    units = gate_weights.shape[2]
    local_heads = features // HEAD
    heads = shards * local_heads
    count = extent[0, 0] * extent[0, 1]
    block = 256
    blocks = rows // block

    def each_block(step):
        def run(i, _):
            step(i * block, pl.ds(aligned(i * block, block), block))
            return 0

        lax.fori_loop(0, blocks, run, 0)

    sources = (None, output_source, gate_source, up_source, down_source)
    places = (attention_weights, output_weights, gate_weights, up_weights, down_weights)
    owned = [
        pltpu.make_async_copy(source, place.at[mp], local_sem.at[i])
        for i, (source, place) in enumerate(zip(sources[1:], places[1:]))
    ]
    owned.append(pltpu.make_async_copy(upstream, out_low, local_sem.at[4]))
    turned = [
        pltpu.make_async_copy(source, attention_weights.at[mp, i], local_sem.at[5 + i])
        for i, source in enumerate((query_source, key_source, value_source))
    ]
    peers = [(flip(dp, j), mp) for j in range(1, GROUP)]
    peers += [(dp, flip(mp, k)) for k in range(1, shards)]
    semaphore = announce(peers)
    for copy in turned + owned:
        copy.start()
    for copy in turned:
        copy.wait()
    own_weights[...] = attention_weights[mp].reshape(3 * features, depth).T
    pl.semaphore_wait(semaphore, len(peers))
    gather = Gather(sources, places, send_z, recv_z, send_x, recv_x, send_c, recv_c)
    jobs = [(kind, k) for kind in (0, 1) for k in range(1, shards)]
    jobs += [(kind, k) for k in range(1, shards) for kind in (2, 3, 4)]
    steps = gather.schedule(jobs)
    position = [0]
    clock = [0.0]

    def advance(stop):
        for step in steps[position[0] : stop]:
            step[1]()
        position[0] = max(position[0], stop)

    def pause(spent):
        clock[0] += spent
        advance(sum(step[0] <= clock[0] for step in steps))

    def until(job):
        where = [i for i, step in enumerate(steps) if step[3] and step[2] == job][0]
        clock[0] = max(clock[0], steps[where][0])
        advance(where + 1)

    def gain_of(ref):
        return ref[...].astype(f32).reshape(1, depth)

    def normalise(first, at):
        values = inputs[at, :].astype(f32)
        root = lax.rsqrt(jnp.mean(values * values, axis=-1, keepdims=True) + EPSILON)
        normed_one[at, :] = (values * root * gain_of(first_gain)).astype(bf16)

    each_block(normalise)
    pause(1.5)

    def join(first, at):
        every_output = output_weights[...].reshape(depth, depth)
        values = inputs[at, :].astype(f32) + dot(context[:, at], every_output, 0, 0)
        hidden[at, :] = values
        root = lax.rsqrt(jnp.mean(values * values, axis=-1, keepdims=True) + EPSILON)
        normed_two[at, :] = (values * root * gain_of(second_gain)).astype(bf16)
        out_low[at, :] = jnp.where(row_keep(count, first, block), out_low[at, :], jnp.zeros((), bf16))

    def attention(probs, scores, keys):
        def probs_copy(slot, number):
            return pltpu.make_async_copy(probs.at[slot], probs_out.at[number], probs_sem.at[slot])

        done = 0
        for k in range(shards):
            shard = flip(mp, k)
            if k > 0:
                until((0, k))
            project(attention_weights, normed_one, qkv, shard)
            pause(1.8)
            for head in range(local_heads):
                slot = done % 2
                number = shard * local_heads + head
                if done >= 2:
                    probs_copy(slot, number).wait()
                attend(
                    qkv,
                    shard,
                    head,
                    count,
                    probs.at[slot],
                    context,
                    scale,
                    scores,
                    keys,
                    local_heads,
                    pause,
                )
                probs_copy(slot, number).start()
                done += 1
        pltpu.make_async_copy(attention_weights, weights_out, out_sem.at[0]).start()
        owned[0].wait()
        owned[4].wait()
        for k in range(1, shards):
            until((1, k))
        each_block(join)
        pause(2.4)
        for slot in (done % 2, (done + 1) % 2):
            probs_copy(slot, 0).wait()

    pl.run_scoped(
        attention,
        pltpu.VMEM((2, rows, rows), bf16),
        pltpu.VMEM((2, rows, block), f32),
        pltpu.VMEM((rows, 2 * HEAD), bf16),
    )

    slices = wide_grad.shape[:3]

    def feed_forward(forward_sum, back_sum, mixed_own, gate_own, up_own):
        def feed(shard, k):
            def step(first, at):
                normed, low = normed_two[at, :], out_low[at, :]
                gate = dot(normed, gate_weights[shard], 1, 0)
                up = dot(normed, up_weights[shard], 1, 0)
                mixed_back = dot(low, down_weights[shard], 1, 1)
                bent, slope = gelu_parts(gate)
                mixed = (bent * up).astype(bf16)
                gate_back = (mixed_back * up * slope).astype(bf16)
                up_back = (mixed_back * bent).astype(bf16)
                ahead = dot(mixed, down_weights[shard], 1, 0)
                back = dot(gate_back, gate_weights[shard], 1, 1)
                back = back + dot(up_back, up_weights[shard], 1, 1)
                if k == 0:
                    mixed_own[at, :] = mixed
                    gate_own[at, :] = gate_back
                    up_own[at, :] = up_back
                    forward_sum[at, :] = ahead
                    back_sum[at, :] = back
                else:
                    forward_sum[at, :] += ahead
                    back_sum[at, :] += back

            each_block(step)

        for k in range(shards):
            if k == 0:
                for copy in owned[1:4]:
                    copy.wait()
            else:
                for kind in (2, 3, 4):
                    until((kind, k))
            feed(flip(mp, k), k)
            pause(6.0)
            if k == 0:
                pairs = ((normed_two, gate_own), (normed_two, up_own), (out_low, mixed_own))
                for i, (left, right) in enumerate(pairs):
                    part = dot(left[...], right[...], 0, 0).astype(bf16)
                    wide_grad[:, :, :, i * units : (i + 1) * units] = part.reshape(*slices, units)
                    pause(0.9)
        advance(len(steps))

        def close(first, at):
            keep = row_keep(count, first, block)
            values, back = hidden[at, :], back_sum[at, :]
            out_back = out_low[at, :].astype(f32)
            out_low[at, :] = jnp.where(keep, values + forward_sum[at, :], 0.0).astype(bf16)
            root = lax.rsqrt(jnp.mean(values * values, axis=-1, keepdims=True) + EPSILON)
            scaled = gain_of(second_gain) * back
            mean = jnp.mean(scaled * values, axis=-1, keepdims=True)
            result = out_back + root * scaled - values * (root * root * root * mean)
            hidden[at, :] = result
            normed_two[at, :] = result.astype(bf16)

        each_block(close)

    pl.run_scoped(
        feed_forward,
        pltpu.VMEM((rows, depth), f32),
        pltpu.VMEM((rows, depth), f32),
        pltpu.VMEM((rows, units), bf16),
        pltpu.VMEM((rows, units), bf16),
        pltpu.VMEM((rows, units), bf16),
    )
    pltpu.make_async_copy(out_low, layer_output, out_sem.at[1]).start()
    pltpu.make_async_copy(hidden, hidden_out, out_sem.at[2]).start()
    hidden_low = normed_two
    own = context[pl.ds(aligned(mp * features, HEAD), features), :]
    part = dot(own, hidden_low[...], 1, 0).T.astype(bf16)
    wide_grad[:, :, :, 3 * units :] = part.reshape(*slices, features)
    wide = Reduce(wide_grad, wide_core, wide_chips, wide_total, wide_sem)
    narrow = Reduce(narrow_grad, narrow_core, narrow_chips, narrow_total, narrow_sem)
    wide.begin()

    def context_step(first, at):
        every_output = output_weights[...].reshape(depth, depth)
        back = dot(every_output, hidden_low[at, :], 1, 1).reshape(heads, HEAD, block)
        low = (back * scale[:, :, at]).astype(bf16)
        context_back[:, at] = low.reshape(depth, block)
        ahead = context[:, at].reshape(heads, HEAD, block).astype(f32)
        delta[:, :, at] = jnp.sum(low.astype(f32) * ahead, axis=1, keepdims=True)

    each_block(context_step)

    def gains_copy(k):
        return pltpu.make_async_remote_copy(
            src_ref=gains_own,
            dst_ref=gains_in.at[k - 1],
            send_sem=gains_sem.at[0, k],
            recv_sem=gains_sem.at[1, k],
            device_id=(dp, flip(mp, k)),
            device_id_type=MESH,
        )

    def gains():
        piece = gains_own.shape[0]
        at = pl.ds(aligned((dp % GROUP) * piece, 32), piece)
        second = gate_weights[mp, at, :].astype(f32) * wide_total[:, :units]
        second = second + up_weights[mp, at, :].astype(f32) * wide_total[:, units : 2 * units]
        first = own_weights[at, :].astype(f32) * narrow_total[...]
        lane = lax.broadcasted_iota(jnp.int32, gains_own.shape, 1)
        first = jnp.sum(first, axis=1, keepdims=True)
        second = jnp.sum(second, axis=1, keepdims=True)
        gains_own[...] = jnp.where(lane == 0, first, jnp.where(lane == 1, second, 0.0))
        for k in range(1, shards):
            gains_copy(k).start()

    def attention_back(probs, score_back, grads):
        def fetch(i):
            number = cross(mp, i // local_heads) * local_heads + i % local_heads
            return pltpu.make_async_copy(probs_out.at[number], probs.at[i % 2], probs_sem.at[i % 2])

        def keep_grads(shard, k):
            return pltpu.make_async_copy(grads.at[shard], grads_out.at[shard], grads_sem.at[k])

        def step(i, _):
            k, head = i // local_heads, i % local_heads
            shard = cross(mp, k)
            fetch(i).wait()

            @pl.when(i + 1 < heads)
            def _():
                fetch(i + 1).start()

            attend_back(
                qkv,
                grads,
                shard,
                head,
                probs.at[i % 2],
                context_back,
                delta,
                score_back,
                local_heads,
            )

            @pl.when(head == local_heads - 1)
            def _():
                keep_grads(shard, k).start()

            @pl.when(i == local_heads - 1)
            def _():
                wide.middle()
                part = dot(grads[mp], normed_one[...], 1, 0).T.astype(bf16)
                narrow_grad[...] = part.reshape(narrow_grad.shape)
                narrow.begin()

            @pl.when(i == local_heads)
            def _():
                narrow.middle()

            @pl.when(i == heads - 2)
            def _():
                wide.end()
                narrow.end()
                gains()

            return 0

        fetch(0).start()
        lax.fori_loop(0, heads, step, 0)
        for k in range(shards):
            keep_grads(flip(mp, k), k).wait()

    pl.run_scoped(
        attention_back,
        pltpu.VMEM((2, rows, rows), bf16),
        pltpu.VMEM((rows, rows), bf16),
        pltpu.VMEM((shards, 3 * features, rows), bf16),
    )
    for k in range(1, shards):
        gains_copy(k).wait()
    gains_total[...] = (gains_own[...] + gains_in[0]) + (gains_in[1] + gains_in[2])
    pltpu.make_async_copy(attention_weights, weights_out, out_sem.at[0]).wait()
    pltpu.make_async_copy(out_low, layer_output, out_sem.at[1]).wait()
    pltpu.make_async_copy(hidden, hidden_out, out_sem.at[2]).wait()
    gather.finish()


def close_kernel(
    grads,
    weights,
    hidden_back,
    inputs,
    first_gain,
    layer_in,
    wide_total,
    narrow_total,
    input_grad,
    layer_output,
    query_grad,
    key_grad,
    value_grad,
    output_grad,
    gate_grad,
    up_grad,
    down_grad,
):
    shards, narrow, block = grads.shape
    depth = inputs.shape[1]
    values = inputs[...].astype(f32)
    every_weight = weights[...].reshape(shards * narrow, depth)
    back = dot(grads[...].reshape(shards * narrow, block), every_weight, 0, 0)
    root = lax.rsqrt(jnp.mean(values * values, axis=-1, keepdims=True) + EPSILON)
    scaled = first_gain[...].astype(f32).reshape(1, depth) * back
    mean = jnp.mean(scaled * values, axis=-1, keepdims=True)
    result = hidden_back[...] + root * scaled
    input_grad[...] = result - values * (root * root * root * mean)
    layer_output[...] = layer_in[...]

    @pl.when(pl.program_id(0) == 0)
    def _():
        features, units = query_grad.shape[1], gate_grad.shape[1]
        query_grad[...] = narrow_total[:, :features]
        key_grad[...] = narrow_total[:, features : 2 * features]
        value_grad[...] = narrow_total[:, 2 * features :]
        gate_grad[...] = wide_total[:, :units]
        up_grad[...] = wide_total[:, units : 2 * units]
        down_grad[...] = wide_total[:, 2 * units : 3 * units].T
        output_grad[...] = wide_total[:, 3 * units :].T


def vmem():
    return pl.BlockSpec(memory_space=pltpu.VMEM)


def anywhere():
    return pl.BlockSpec(memory_space=pl.ANY)


def body(groups, shards, *arguments):
    (
        patches,
        attention_gain,
        query_weight,
        key_weight,
        value_weight,
        output_weight,
        feedforward_gain,
        gate_weight,
        up_weight,
        down_weight,
        cotangent,
        grid_extent,
    ) = arguments
    rows, depth = patches.shape
    features, units = query_weight.shape[1], gate_weight.shape[1]
    heads = shards * features // HEAD
    piece = depth // GROUP
    wide, narrow = 3 * units + features, 3 * features

    shape = jax.ShapeDtypeStruct
    kinds = Gather.KINDS
    dma = pltpu.SemaphoreType.DMA
    (
        layer_output,
        _,
        grads,
        weights,
        hidden_back,
        wide_total,
        narrow_total,
        gains_total,
    ) = pl.pallas_call(
        main_kernel,
        name="layer",
        out_shape=(
            shape((rows, depth), bf16),
            shape((heads, rows, rows), bf16),
            shape((shards, narrow, rows), bf16),
            shape((shards, 3, features, depth), bf16),
            shape((rows, depth), f32),
            shape((piece, wide), f32),
            shape((piece, narrow), f32),
            shape((piece, 128), f32),
        ),
        in_specs=[pl.BlockSpec(memory_space=pltpu.SMEM)] + [vmem()] * 3 + [anywhere()] * 8,
        out_specs=(anywhere(),) * 5 + (vmem(),) * 3,
        scratch_shapes=[
            pltpu.VMEM((shards, 3, features, depth), bf16),
            pltpu.VMEM((shards, features, depth), bf16),
            pltpu.VMEM((shards, depth, units), bf16),
            pltpu.VMEM((shards, depth, units), bf16),
            pltpu.VMEM((shards, units, depth), bf16),
            pltpu.VMEM((shards, narrow, rows), bf16),
            pltpu.VMEM((depth, rows), bf16),
            pltpu.VMEM((rows, depth), bf16),
            pltpu.VMEM((rows, depth), bf16),
            pltpu.VMEM((rows, depth), bf16),
            pltpu.VMEM((rows, depth), f32),
            pltpu.VMEM((heads, 1, rows), f32),
            pltpu.VMEM((heads, 1, rows), f32),
            pltpu.VMEM((depth, rows), bf16),
            pltpu.VMEM((4, 2, piece, wide), bf16),
            pltpu.VMEM((4, 2, piece, narrow), bf16),
            pltpu.VMEM((4, piece, wide), bf16),
            pltpu.VMEM((3, piece, wide), bf16),
            pltpu.VMEM((4, piece, narrow), bf16),
            pltpu.VMEM((3, piece, narrow), bf16),
            pltpu.VMEM((piece, 128), f32),
            pltpu.VMEM((3, piece, 128), f32),
            pltpu.VMEM((depth, narrow), bf16),
            dma((8,)),
            dma((2,)),
            dma((3,)),
            dma((shards,)),
            dma((2, 4)),
            dma((2, 4)),
            dma((2, shards)),
            dma((kinds, shards)),
            dma((kinds, shards)),
            dma((kinds, shards, 4)),
            dma((kinds, shards, 4)),
            dma((kinds, shards, 4)),
            dma((kinds, shards, 4)),
        ],
        compiler_params=pltpu.CompilerParams(
            collective_id=0, has_side_effects=True, vmem_limit_bytes=VMEM_LIMIT
        ),
    )(
        grid_extent,
        patches,
        attention_gain,
        feedforward_gain,
        cotangent,
        query_weight.T,
        key_weight.T,
        value_weight.T,
        output_weight,
        gate_weight,
        up_weight,
        down_weight,
    )

    block = 256

    def whole(*dims):
        return pl.BlockSpec(dims, lambda i: (0,) * len(dims))

    by_rows = pl.BlockSpec((block, depth), lambda i: (i, 0))
    small = [(piece, features)] * 3 + [(features, piece)] + [(piece, units)] * 2 + [(units, piece)]
    input_grad, layer_output, *small_grads = pl.pallas_call(
        close_kernel,
        name="close",
        grid=(rows // block,),
        out_shape=[shape((rows, depth), f32), shape((rows, depth), bf16)]
        + [shape(dims, f32) for dims in small],
        in_specs=[
            pl.BlockSpec((shards, narrow, block), lambda i: (0, 0, i)),
            whole(shards, 3, features, depth),
            by_rows,
            by_rows,
            whole(depth),
            by_rows,
            whole(piece, wide),
            whole(piece, narrow),
        ],
        out_specs=[by_rows, by_rows] + [whole(*dims) for dims in small],
        compiler_params=pltpu.CompilerParams(vmem_limit_bytes=VMEM_LIMIT),
    )(grads, weights, hidden_back, patches, attention_gain, layer_output, wide_total, narrow_total)

    index = lax.axis_index("dp")
    gains_total = gains_total[:, :2]
    if groups > 1:

        def spread(block, turned=False):
            block = block.T if turned else block
            whole = jnp.zeros((depth, block.shape[1]), f32)
            whole = lax.dynamic_update_slice(whole, block, ((index % GROUP) * piece, 0))
            own = lax.psum_scatter(whole, "dp", scatter_dimension=0, tiled=True)
            return own.T if turned else own

        small_grads = [spread(grad, i in (3, 6)) for i, grad in enumerate(small_grads)]
        gains_total = spread(gains_total)
    kept = depth // (groups * GROUP)

    def gain_grad(column, gain):
        own = lax.dynamic_slice_in_dim(gain.astype(f32), index * kept, kept)
        return gains_total[:, column] / own

    query_grad, key_grad, value_grad, output_grad, gate_grad, up_grad, down_grad = small_grads
    return (
        layer_output,
        input_grad,
        gain_grad(0, attention_gain),
        query_grad,
        key_grad,
        value_grad,
        output_grad,
        gain_grad(1, feedforward_gain),
        gate_grad,
        up_grad,
        down_grad,
    )


def solution(mesh):
    placed = (
        P("dp", None),
        P(),
        P(None, "mp"),
        P(None, "mp"),
        P(None, "mp"),
        P("mp", None),
        P(),
        P(None, "mp"),
        P(None, "mp"),
        P("mp", None),
        P("dp", None),
        P("dp", None),
    )
    return jax.shard_map(
        functools.partial(body, mesh.shape["dp"] // GROUP, mesh.shape["mp"]),
        mesh=mesh,
        in_specs=placed,
        out_specs=(
            P("dp", None),
            P("dp", None),
            P("dp"),
            P("dp", "mp"),
            P("dp", "mp"),
            P("dp", "mp"),
            P("mp", "dp"),
            P("dp"),
            P("dp", "mp"),
            P("dp", "mp"),
            P("mp", "dp"),
        ),
        check_vma=False,
    )
```

time: 1000 us -> 142 us (0.14)
  waiting for transfers between devices: 815 us -> 0 us
  Pallas kernels: 0 us -> 139 us
  matrix products: 75.7 us -> 0 us
  other arithmetic: 32.9 us -> 0.61 us
  local copies, waits for them, and re-layouts: 27.9 us -> 1.95 us
  between operations: 17.2 us -> 0.72 us
  blocking collectives: 12.6 us -> 0 us
  loops' own time: 12.1 us -> 0 us
    reduce_scatter x11 -> x0, waiting for transfers between devices: 520 us -> none  [the longest x1 63.1 us: attention_repeat(): lax.psum_scatter(partial_value, 'mp', scatter_dimension=0, tiled=True)]
    all_gather x5 -> x0, waiting for transfers between devices: 279 us -> none  [the longest x1 65.1 us: body(): normed_one_back = lax.all_gather(normed_one_share, 'mp', axis=0, tiled=True)]
    pallas_call x0 -> x2, Pallas kernels: none -> 139 us  [the longest x1 128 us: body(): pl.pallas_call(main_kernel, name='layer', out_shape=(shape((rows, depth),...]
    dot_general x40 -> x0, matrix products: 72.2 us -> none  [the longest x6 9.25 us: block_scores(): jnp.einsum('qhd,khd->hqk', query_block, keys_all, preferred_element_type=...]
    reduce_sum x9 -> x0, other arithmetic: 22.7 us -> none  [the longest x3 9.95 us: rms_scale(): jnp.mean(values * values, axis=-1, keepdims=True) + epsilon]
    unnamed x18 -> x0, waiting for transfers between devices: 16.6 us -> none
    unnamed x134 -> x7, local copies, waits for them, and re-layouts: 15.4 us -> 1.77 us
    unnamed x1 -> x0, blocking collectives: 12.6 us -> none
  transfers between devices with their start and end apart: 17 -> 0, of which waited for: 17 -> 0; matrix products, arithmetic and copies ran while one was open for 4% -> 0% of each run, Pallas kernels for 0% -> 0%
where the time goes in v1:
time: 142 us
  Pallas kernels  139 us (98%)
  local copies, waits for them, and re-layouts  1.95 us (1%)
    pallas_call x1, Pallas kernels, body(): pl.pallas_call(main_kernel, name='layer', out_shape=(shape((rows, depth),...  128 us
    pallas_call x1, Pallas kernels, body(): pl.pallas_call(close_kernel, name='close', grid=(rows // block,), out_sha...  11.1 us

profile of v1, /device:TPU:0, one launch (start us, length us, event | category | flops | bytes accessed | tf_op | source)
XLA Modules:
  0.0 142.2 jit_solution(13564987400337633702)
XLA Ops:
  0.6 127.8 %layer.1 = (bf16[1024,768]{1,0:T(8,128)(2,1)}, bf16[12,1024,1024]{2,1,0:T(8,128)(2,1)}, bf16[4,576,1024]{2,1,0:T(8,128)(2,1)}, bf16[4,3,192,768]{3,2,1,0:T(8,128...) custom-call(s32[1,2]{1,0:T(1,128)} %extent.1, ...), custom_call_target="tpu_custom_call" | custom-call | tf_op jit(solution)/shard_map/layer/pallas_call | solution.py:755
  128.5 0.0 copy-start
  128.5 0.0 copy-start.1
  128.5 0.0 copy-start.2
  128.5 11.1 %close.1 = (f32[1024,768]{1,0:T(8,128)}, bf16[1024,768]{1,0:T(8,128)(2,1)}, f32[96,192]{1,0:T(8,128)}, f32[96,192]{1,0:T(8,128)}, f32[96,192]{1,0:T(8,128)}, /*i...) custom-call(bf16[4,576,1024]{2,1,0:T(8,128)(2,1)} %get-tuple-element.27.grads, ...), custom_call_target="tpu_custom_call" | custom-call | tf_op jit(solution)/shard_map/close/pallas_call | solution.py:833
  139.6 1.8 %copy.24 = f32[512,96]{0,1:T(8,128)} copy(f32[512,96]{1,0:T(8,128)} %get-tuple-element.64) | data formatting | bytes 393216
  141.4 0.0 copy-done
  141.4 0.2 slice_reduce_fusion
  141.6 0.0 copy-done.1
  141.6 0.0 copy-done.2
  141.6 0.6 dynamic-slice_divide_fusion
  (2 shorter events, 0.0 us)
Async XLA Ops:
  128.5 12.9 %copy-start = (f32[96,128]{1,0:T(8,128)S(1)}, f32[96,128]{1,0:T(8,128)}, u32[]{:S(2)}) copy-start(f32[96,128]{1,0:T(8,128)} %get-tuple-element.35) | copy-start | bytes 147460
  128.5 13.1 %copy-start.1 = (bf16[768]{0:T(1024)(128)(2,1)S(1)}, bf16[768]{0:T(1024)(128)(2,1)}, u32[]{:S(2)}) copy-start(bf16[768]{0:T(1024)(128)(2,1)} %first_gain.3) | copy-start | bytes 4612
  128.5 13.1 %copy-start.2 = (bf16[768]{0:T(1024)(128)(2,1)S(1)}, bf16[768]{0:T(1024)(128)(2,1)}, u32[]{:S(2)}) copy-start(bf16[768]{0:T(1024)(128)(2,1)} %second_gain.1) | copy-start | bytes 4612
